TPU v7x, 256 devices: a whole 4x4x8 slice. The times are simulated.
256 devices in a mesh: row: 64 (over y, x_hi, z), col: 4 (over x_lo, core).
Axes of the slice: x: 4 (x_hi: 2, x_lo: 2; x = x_hi * 2 + x_lo), y: 4, z: 8, core: 2. Of those that a mesh axis runs over, the one named last changes fastest.
Arguments:
- operator: bfloat16 [32768, 32768], P('row', 'col'), may hold values from -0.0068359375 to 0.0068359375
- rhs: float32 [32, 32768], P(None, 'row'), may hold values from -72 to 72
- bodies: int32 [32768], P('row'), may hold values from 0 to 63, as said below
- weights: float32 [32768], P('row'), may hold values from 0.5 to 1.5
Outputs:
- basis: float32 [128, 32768], P(None, ('row', 'col'))
- hess: float32 [128, 96], replicated
- start_factor: float32 [32, 32], replicated
Inputs may be any that keep to these rules, and one draw needn't show every extreme that they name: Every one of the 64 bodies has at least one node.
All inputs are finite; a program needn't handle non-finite values.
Results may differ from a plain program's by a relative error of at most 0.0025.
Values may be sent and summed in bfloat16 or wider, within the bound.
A program may use at most 64 MiB of HBM per device.

v0:
```python
import jax
import jax.numpy as jnp
from jax import lax
from jax.sharding import Mesh
from jax.sharding import PartitionSpec as P

N = 32768
S = 32
BODIES = 64
STEPS = 3
COL = ("col_0", "col_1")
ROW_COL = ("row_0", "row_1", "row_2", "col_0", "col_1")
ROW = ("row_0", "row_1", "row_2")


def one_axis_at_a_time(shard, axes):
    for axis in axes:
        shard = lax.psum(shard, axis)
    return shard


def joined_along(parts, dim):
    parts = jnp.moveaxis(parts, 0, dim)
    lengths = parts.shape
    return parts.reshape(*lengths[:dim], lengths[dim] * lengths[dim + 1], *lengths[dim + 2 :])


def all_blocks(shard, axes, sequence):
    parts = shard
    for k in sequence:
        parts = lax.all_gather(parts, axes[k])
    done = sequence[::-1]
    back = [done.index(k) for k in range(len(axes))]
    parts = parts.transpose(*back, *range(len(axes), parts.ndim))
    return parts.reshape(-1, *shard.shape)


def whole_of(shard, axes, sequence, dim):
    return joined_along(all_blocks(shard, axes, sequence), dim)


def sent_to_all(shard, axis):
    copies = jnp.broadcast_to(shard, (lax.axis_size(axis), *shard.shape))
    return lax.all_to_all(copies, axis, split_axis=0, concat_axis=0, tiled=True)


def over_copies(shard, axis):
    everything = sent_to_all(shard, axis)
    return jnp.sum(everything, axis=0)


def product_t(left, right):
    return lax.dot_general(
        left,
        right,
        (((1,), (1,)), ((), ())),
        precision=lax.Precision.HIGHEST,
        preferred_element_type=jnp.float32,
    )


def local(operator, rhs, bodies, weights):
    col_index = lax.axis_index(COL)
    col_count = lax.axis_size(COL)
    row_width = rhs.shape[1]
    quarter = row_width // col_count

    def portion(values):
        return lax.dynamic_slice_in_dim(values, col_index * quarter, quarter, 1)

    onehot = (bodies[:, None] == jnp.arange(BODIES, dtype=jnp.int32)[None, :]).astype(jnp.float32)
    onehot_part = jnp.transpose(portion(onehot.T))
    gram_start = one_axis_at_a_time(product_t(portion(rhs), portion(rhs)), ROW_COL) / N
    start_low = jnp.linalg.cholesky(gram_start)
    basis_list = [lax.linalg.triangular_solve(start_low, rhs, left_side=True, lower=True)]
    col_width = operator.shape[1]
    columns = []
    for step_index in range(STEPS):
        current = basis_list[-1]
        current_low = current.astype(jnp.bfloat16)
        gathered = whole_of(current_low, ROW, (1, 2, 0), 1)
        col_block = lax.dynamic_slice_in_dim(gathered, col_index * col_width, col_width, 1)
        partial_terms = lax.dot_general(
            col_block, operator, (((1,), (1,)), ((), ())), preferred_element_type=jnp.float32
        )
        coupled = over_copies(partial_terms, COL)
        scaled = current_low.astype(jnp.float32) * weights[None, :]
        body_partial = jnp.dot(portion(scaled), onehot_part, precision=lax.Precision.HIGHEST)
        body_means = one_axis_at_a_time(body_partial, ROW_COL) * (BODIES / N)
        completion = weights[None, :] * product_t(body_means, onehot)
        image_block = 0.5 * current + coupled + completion
        stacked = jnp.concatenate(basis_list, axis=0)
        stacked_part = portion(stacked)
        image_part = portion(image_block)
        coef_raw, gram_raw = (
            one_axis_at_a_time(product_t(stacked_part, image_part), ROW_COL),
            one_axis_at_a_time(product_t(image_part, image_part), ROW_COL),
        )
        first_coef = coef_raw / N
        residual_one = image_block - jnp.dot(first_coef.T, stacked, precision=lax.Precision.HIGHEST)
        gram_block = gram_raw / N - jnp.dot(
            first_coef.T, first_coef, precision=lax.Precision.HIGHEST
        )
        factor_low = jnp.linalg.cholesky(gram_block)
        basis_list.append(
            lax.linalg.triangular_solve(factor_low, residual_one, left_side=True, lower=True)
        )
        pieces = [first_coef, factor_low.T]
        below = (STEPS - 1 - step_index) * S
        if below > 0:
            pieces.append(jnp.zeros((below, S), jnp.float32))
        columns.append(jnp.concatenate(pieces, axis=0))
    basis = portion(jnp.concatenate(basis_list, axis=0))
    return (basis, jnp.concatenate(columns, axis=1), start_low)


def solution(mesh):
    split = Mesh(mesh.devices.reshape(4, 2, 8, 2, 2), ("row_0", "row_1", "row_2", "col_0", "col_1"))
    placed = (P(ROW, COL), P(None, ROW), P(ROW), P(ROW))
    return jax.shard_map(
        local, mesh=split, in_specs=placed, out_specs=(P(None, ROW_COL), P(), P()), check_vma=False
    )
```

profile of v0, /device:TPU:1, one launch (start us, length us, event | category | flops | bytes accessed | tf_op | source)
XLA Modules:
  0.0 710.6 jit_solution(9784179976770746269)
XLA Ops:
  8.2 14.2 %psum.350 = f32[32,32]{0,1:T(8,128)S(1)} all-reduce(f32[32,32]{0,1:T(8,128)S(1)} %fusion.50), channel_id=1, replica_groups=mesh['row_0'=4,'row_1'=2,'row_2'=8,'col_0'=2,'col_1'=2] {'row_0'}, use_global_device_ids=true, to_apply=%region_0.0 | all-reduce | flops 1024 | bytes 8192 | tf_op jit(solution)/shard_map/psum | solution.py:18
  22.4 9.1 %psum.351 = f32[32,32]{0,1:T(8,128)S(1)} all-reduce(f32[32,32]{0,1:T(8,128)S(1)} %psum.350), channel_id=1, replica_groups=mesh['row_0'=4,'row_1'=2,'row_2'=8,'col_0'=2,'col_1'=2] {'row_1'}, use_global_device_ids=true, to_apply=%region_1.0 | all-reduce | flops 1024 | bytes 8192 | tf_op jit(solution)/shard_map/psum | solution.py:18
  31.5 25.5 %psum.352 = f32[32,32]{0,1:T(8,128)S(1)} all-reduce(f32[32,32]{0,1:T(8,128)S(1)} %psum.351), channel_id=1, replica_groups=mesh['row_0'=4,'row_1'=2,'row_2'=8,'col_0'=2,'col_1'=2] {'row_2'}, use_global_device_ids=true, to_apply=%region_2.0 | all-reduce | flops 1024 | bytes 8192 | tf_op jit(solution)/shard_map/psum | solution.py:18
  62.2 18.9 %psum.354 = f32[32,32]{0,1:T(8,128)S(1)} all-reduce(f32[32,32]{0,1:T(8,128)S(1)} %psum.353), channel_id=1, replica_groups=mesh['row_0'=4,'row_1'=2,'row_2'=8,'col_0'=2,'col_1'=2] {'col_1'}, use_global_device_ids=true, to_apply=%region_4.0 | all-reduce | flops 1024 | bytes 8192 | tf_op jit(solution)/shard_map/psum | solution.py:18
  93.7 21.4 %all-gather.1 = bf16[16,32,512]{2,1,0:T(8,128)(2,1)} all-gather(bf16[2,32,512]{2,1,0:T(8,128)(2,1)S(1)} %bitcast.98), channel_id=3, replica_groups=mesh['row_0'=4,'row_1'=2,'row_2'=8,'col_0'=2,'col_1'=2] {'row_2'}, dimensions={0}, use_global_device_ids=true | all-gather | bytes 589824 | tf_op jit(solution)/shard_map/all_gather | solution.py:31
  116.8 33.1 %all-gather.13.cloned.1.call-done = bf16[32,2,32,512]{3,2,1,0:T(8,128)(2,1)} async-done(((bf16[8,2,32,512]{3,2,1,0:T(8,128)(2,1)}), bf16[32,2,32,512]{3,2,1,0:T(8,128)(2,1)}) %all-gather.13.cloned.1.call-update) | async-done | bytes 2097168 | tf_op jit(solution)/shard_map/all_gather | solution.py:31
  161.6 11.2 %psum.355 = f32[32,64]{1,0:T(8,128)S(1)} all-reduce(f32[32,64]{1,0:T(8,128)S(1)} %fusion.24), channel_id=1, replica_groups=mesh['row_0'=4,'row_1'=2,'row_2'=8,'col_0'=2,'col_1'=2] {'row_0'}, use_global_device_ids=true, to_apply=%region_8.11 | all-reduce | flops 2048 | bytes 16384 | tf_op jit(solution)/shard_map/psum | solution.py:18
  172.8 9.1 %psum.356 = f32[32,64]{1,0:T(8,128)S(1)} all-reduce(f32[32,64]{1,0:T(8,128)S(1)} %psum.355), channel_id=1, replica_groups=mesh['row_0'=4,'row_1'=2,'row_2'=8,'col_0'=2,'col_1'=2] {'row_1'}, use_global_device_ids=true, to_apply=%region_9.12 | all-reduce | flops 2048 | bytes 16384 | tf_op jit(solution)/shard_map/psum | solution.py:18
  181.9 23.3 %psum.357 = f32[32,64]{1,0:T(8,128)S(1)} all-reduce(f32[32,64]{1,0:T(8,128)S(1)} %psum.356), channel_id=1, replica_groups=mesh['row_0'=4,'row_1'=2,'row_2'=8,'col_0'=2,'col_1'=2] {'row_2'}, use_global_device_ids=true, to_apply=%region_10.13 | all-reduce | flops 2048 | bytes 16384 | tf_op jit(solution)/shard_map/psum | solution.py:18
  211.0 18.1 %psum.359 = f32[32,64]{1,0:T(8,128)S(1)} all-reduce(f32[32,64]{1,0:T(8,128)S(1)} %psum.358), channel_id=1, replica_groups=mesh['row_0'=4,'row_1'=2,'row_2'=8,'col_0'=2,'col_1'=2] {'col_1'}, use_global_device_ids=true, to_apply=%region_12.15 | all-reduce | flops 2048 | bytes 16384 | tf_op jit(solution)/shard_map/psum | solution.py:18
  229.9 11.3 %all-reduce.5 = (f32[32,32]{0,1:T(8,128)S(1)}, f32[32,32]{0,1:T(8,128)S(1)}) all-reduce(f32[32,32]{0,1:T(8,128)S(1)} %fusion.45, f32[32,32]{0,1:T(8,128)S(1)} %fusion.59), channel_id=1, replica_groups=mesh['row_0'=4,'row_1'=2,'row_2'=8,'col_0'=2,'col_1'=2] {'row_0'}, use_global_device_ids=true, to_apply=%region_18.21 | all-reduce | flops 2048 | bytes 16384 | tf_op jit(solution)/shard_map/psum | solution.py:18
  241.2 8.1 %all-reduce.14 = (f32[32,32]{0,1:T(8,128)S(1)}, f32[32,32]{0,1:T(8,128)S(1)}) all-reduce(f32[32,32]{0,1:T(8,128)S(1)} %get-tuple-element.15, f32[32,32]{0,1:T(8,128)S(1)} %get-tuple-element.16), channel_id=1, replica_groups=mesh['row_0'=4,'row_1'=2,'row_2'=8,'col_0'=2,'col_1'=2] {'row_1'}, use_global_device_ids=true, to_apply=%region_19.22 | all-reduce | flops 2048 | bytes 16384 | tf_op jit(solution)/shard_map/psum | solution.py:18
  249.3 20.2 %all-reduce.2 = (f32[32,32]{0,1:T(8,128)S(1)}, f32[32,32]{0,1:T(8,128)S(1)}) all-reduce(f32[32,32]{0,1:T(8,128)S(1)} %get-tuple-element.33, f32[32,32]{0,1:T(8,128)S(1)} %get-tuple-element.34), channel_id=1, replica_groups=mesh['row_0'=4,'row_1'=2,'row_2'=8,'col_0'=2,'col_1'=2] {'row_2'}, use_global_device_ids=true, to_apply=%region_20.23 | all-reduce | flops 2048 | bytes 16384 | tf_op jit(solution)/shard_map/psum | solution.py:18
  274.9 17.4 %all-reduce.8 = (f32[32,32]{0,1:T(8,128)S(1)}, f32[32,32]{0,1:T(8,128)S(1)}) all-reduce(f32[32,32]{0,1:T(8,128)S(1)} %get-tuple-element.27, f32[32,32]{0,1:T(8,128)S(1)} %get-tuple-element.28), channel_id=1, replica_groups=mesh['row_0'=4,'row_1'=2,'row_2'=8,'col_0'=2,'col_1'=2] {'col_1'}, use_global_device_ids=true, to_apply=%region_22.25 | all-reduce | flops 2048 | bytes 16384 | tf_op jit(solution)/shard_map/psum | solution.py:18
  304.7 21.7 %all-gather.4 = bf16[16,32,512]{2,1,0:T(8,128)(2,1)} all-gather(bf16[2,32,512]{2,1,0:T(8,128)(2,1)S(1)} %bitcast.99), channel_id=6, replica_groups=mesh['row_0'=4,'row_1'=2,'row_2'=8,'col_0'=2,'col_1'=2] {'row_2'}, dimensions={0}, use_global_device_ids=true | all-gather | bytes 589824 | tf_op jit(solution)/shard_map/all_gather | solution.py:31
  326.5 36.9 %all-gather.15.cloned.1.call-done = bf16[32,2,32,512]{3,2,1,0:T(8,128)(2,1)} async-done(((bf16[8,2,32,512]{3,2,1,0:T(8,128)(2,1)}), bf16[32,2,32,512]{3,2,1,0:T(8,128)(2,1)}) %all-gather.15.cloned.1.call-update) | async-done | bytes 2097168 | tf_op jit(solution)/shard_map/all_gather | solution.py:31
  376.4 11.2 %psum.370 = f32[32,64]{1,0:T(8,128)S(1)} all-reduce(f32[32,64]{1,0:T(8,128)S(1)} %fusion.22), channel_id=1, replica_groups=mesh['row_0'=4,'row_1'=2,'row_2'=8,'col_0'=2,'col_1'=2] {'row_0'}, use_global_device_ids=true, to_apply=%region_24.27 | all-reduce | flops 2048 | bytes 16384 | tf_op jit(solution)/shard_map/psum | solution.py:18
  387.7 9.1 %psum.371 = f32[32,64]{1,0:T(8,128)S(1)} all-reduce(f32[32,64]{1,0:T(8,128)S(1)} %psum.370), channel_id=1, replica_groups=mesh['row_0'=4,'row_1'=2,'row_2'=8,'col_0'=2,'col_1'=2] {'row_1'}, use_global_device_ids=true, to_apply=%region_25.28 | all-reduce | flops 2048 | bytes 16384 | tf_op jit(solution)/shard_map/psum | solution.py:18
  396.8 23.3 %psum.372 = f32[32,64]{1,0:T(8,128)S(1)} all-reduce(f32[32,64]{1,0:T(8,128)S(1)} %psum.371), channel_id=1, replica_groups=mesh['row_0'=4,'row_1'=2,'row_2'=8,'col_0'=2,'col_1'=2] {'row_2'}, use_global_device_ids=true, to_apply=%region_26.29 | all-reduce | flops 2048 | bytes 16384 | tf_op jit(solution)/shard_map/psum | solution.py:18
  425.9 18.1 %psum.374 = f32[32,64]{1,0:T(8,128)S(1)} all-reduce(f32[32,64]{1,0:T(8,128)S(1)} %psum.373), channel_id=1, replica_groups=mesh['row_0'=4,'row_1'=2,'row_2'=8,'col_0'=2,'col_1'=2] {'col_1'}, use_global_device_ids=true, to_apply=%region_28.31 | all-reduce | flops 2048 | bytes 16384 | tf_op jit(solution)/shard_map/psum | solution.py:18
  444.7 11.3 %all-reduce.4 = (f32[64,32]{0,1:T(8,128)S(1)}, f32[32,32]{0,1:T(8,128)S(1)}) all-reduce(f32[64,32]{0,1:T(8,128)S(1)} %fusion.18, f32[32,32]{0,1:T(8,128)S(1)} %fusion.56), channel_id=1, replica_groups=mesh['row_0'=4,'row_1'=2,'row_2'=8,'col_0'=2,'col_1'=2] {'row_0'}, use_global_device_ids=true, to_apply=%region_34.37 | all-reduce | flops 3072 | bytes 24576 | tf_op jit(solution)/shard_map/psum | solution.py:18
  464.2 20.2 %all-reduce.1 = (f32[64,32]{0,1:T(8,128)S(1)}, f32[32,32]{0,1:T(8,128)S(1)}) all-reduce(f32[64,32]{0,1:T(8,128)S(1)} %get-tuple-element.31, f32[32,32]{0,1:T(8,128)S(1)} %get-tuple-element.32), channel_id=1, replica_groups=mesh['row_0'=4,'row_1'=2,'row_2'=8,'col_0'=2,'col_1'=2] {'row_2'}, use_global_device_ids=true, to_apply=%region_36.39 | all-reduce | flops 3072 | bytes 24576 | tf_op jit(solution)/shard_map/psum | solution.py:18
  489.8 17.4 %all-reduce.7 = (f32[64,32]{0,1:T(8,128)S(1)}, f32[32,32]{0,1:T(8,128)S(1)}) all-reduce(f32[64,32]{0,1:T(8,128)S(1)} %get-tuple-element.25, f32[32,32]{0,1:T(8,128)S(1)} %get-tuple-element.26), channel_id=1, replica_groups=mesh['row_0'=4,'row_1'=2,'row_2'=8,'col_0'=2,'col_1'=2] {'col_1'}, use_global_device_ids=true, to_apply=%region_38.41 | all-reduce | flops 3072 | bytes 24576 | tf_op jit(solution)/shard_map/psum | solution.py:18
  519.6 21.7 %all-gather.7 = bf16[16,32,512]{2,1,0:T(8,128)(2,1)} all-gather(bf16[2,32,512]{2,1,0:T(8,128)(2,1)S(1)} %bitcast.100), channel_id=9, replica_groups=mesh['row_0'=4,'row_1'=2,'row_2'=8,'col_0'=2,'col_1'=2] {'row_2'}, dimensions={0}, use_global_device_ids=true | all-gather | bytes 589824 | tf_op jit(solution)/shard_map/all_gather | solution.py:31
  541.5 11.8 %psum.385 = f32[32,64]{1,0:T(8,128)S(1)} all-reduce(f32[32,64]{1,0:T(8,128)S(1)} %fusion.20), channel_id=1, replica_groups=mesh['row_0'=4,'row_1'=2,'row_2'=8,'col_0'=2,'col_1'=2] {'row_0'}, use_global_device_ids=true, to_apply=%region_40.43 | all-reduce | flops 2048 | bytes 16384 | tf_op jit(solution)/shard_map/psum | solution.py:18
  553.3 9.2 %psum.386 = f32[32,64]{1,0:T(8,128)S(1)} all-reduce(f32[32,64]{1,0:T(8,128)S(1)} %psum.385), channel_id=1, replica_groups=mesh['row_0'=4,'row_1'=2,'row_2'=8,'col_0'=2,'col_1'=2] {'row_1'}, use_global_device_ids=true, to_apply=%region_41.44 | all-reduce | flops 2048 | bytes 16384 | tf_op jit(solution)/shard_map/psum | solution.py:18
  562.5 22.1 %psum.387 = f32[32,64]{1,0:T(8,128)S(1)} all-reduce(f32[32,64]{1,0:T(8,128)S(1)} %psum.386), channel_id=1, replica_groups=mesh['row_0'=4,'row_1'=2,'row_2'=8,'col_0'=2,'col_1'=2] {'row_2'}, use_global_device_ids=true, to_apply=%region_42.45 | all-reduce | flops 2048 | bytes 16384 | tf_op jit(solution)/shard_map/psum | solution.py:18
  589.5 23.1 %psum.389 = f32[32,64]{1,0:T(8,128)S(1)} all-reduce(f32[32,64]{1,0:T(8,128)S(1)} %psum.388), channel_id=1, replica_groups=mesh['row_0'=4,'row_1'=2,'row_2'=8,'col_0'=2,'col_1'=2] {'col_1'}, use_global_device_ids=true, to_apply=%region_44.47 | all-reduce | flops 2048 | bytes 16384 | tf_op jit(solution)/shard_map/psum | solution.py:18
  630.9 11.0 %all-reduce.3 = (f32[96,32]{0,1:T(8,128)S(1)}, f32[32,32]{0,1:T(8,128)S(1)}) all-reduce(f32[96,32]{0,1:T(8,128)S(1)} %fusion.15, f32[32,32]{0,1:T(8,128)S(1)} %fusion.53), channel_id=1, replica_groups=mesh['row_0'=4,'row_1'=2,'row_2'=8,'col_0'=2,'col_1'=2] {'row_0'}, use_global_device_ids=true, to_apply=%region_50.53 | all-reduce | flops 4096 | bytes 32768 | tf_op jit(solution)/shard_map/psum | solution.py:18
  641.9 9.1 %all-reduce.12 = (f32[96,32]{0,1:T(8,128)S(1)}, f32[32,32]{0,1:T(8,128)S(1)}) all-reduce(f32[96,32]{0,1:T(8,128)S(1)} %get-tuple-element.11, f32[32,32]{0,1:T(8,128)S(1)} %get-tuple-element.12), channel_id=1, replica_groups=mesh['row_0'=4,'row_1'=2,'row_2'=8,'col_0'=2,'col_1'=2] {'row_1'}, use_global_device_ids=true, to_apply=%region_51.54 | all-reduce | flops 4096 | bytes 32768 | tf_op jit(solution)/shard_map/psum | solution.py:18
  651.1 20.3 %all-reduce = (f32[96,32]{0,1:T(8,128)S(1)}, f32[32,32]{0,1:T(8,128)S(1)}) all-reduce(f32[96,32]{0,1:T(8,128)S(1)} %get-tuple-element.29, f32[32,32]{0,1:T(8,128)S(1)} %get-tuple-element.30), channel_id=1, replica_groups=mesh['row_0'=4,'row_1'=2,'row_2'=8,'col_0'=2,'col_1'=2] {'row_2'}, use_global_device_ids=true, to_apply=%region_52.55 | all-reduce | flops 4096 | bytes 32768 | tf_op jit(solution)/shard_map/psum | solution.py:18
  676.5 18.7 %all-reduce.6 = (f32[96,32]{0,1:T(8,128)S(1)}, f32[32,32]{0,1:T(8,128)S(1)}) all-reduce(f32[96,32]{0,1:T(8,128)S(1)} %get-tuple-element.23, f32[32,32]{0,1:T(8,128)S(1)} %get-tuple-element.24), channel_id=1, replica_groups=mesh['row_0'=4,'row_1'=2,'row_2'=8,'col_0'=2,'col_1'=2] {'col_1'}, use_global_device_ids=true, to_apply=%region_54.57 | all-reduce | flops 4096 | bytes 32768 | tf_op jit(solution)/shard_map/psum | solution.py:18
  (109 shorter events, 139.2 us)
Async XLA Ops:
  7.2 0.8 copy-start
  7.2 142.7 %all-gather.13.cloned.1.call-start = ((), (), s32[]{:S(2)}) async-start(), calls=%async_computation.3 | async-start | bytes 2621440 | tf_op jit(solution)/shard_map/all_gather | solution.py:31
  149.9 4.0 copy-start.1
  153.9 75.3 %copy-start.2 = (s32[512]{0:T(512)S(1)}, s32[512]{0:T(512)}, u32[]{:S(2)}) copy-start(s32[512]{0:T(512)} %param.9) | copy-start | bytes 6148
  153.9 75.3 %copy-start.3 = (f32[512]{0:T(512)S(1)}, f32[512]{0:T(512)}, u32[]{:S(2)}) copy-start(f32[512]{0:T(512)} %param.10) | copy-start | bytes 6148
  157.2 71.9 %all-to-all-start = ((f32[4,32,512]{2,1,0:T(8,128)}), f32[4,32,512]{2,1,0:T(8,128)S(1)}, u32[]{:S(2)}, u32[]{:S(2)}) async-start(f32[4,32,512]{2,1,0:T(8,128)} %broadcast_in_dim.11), calls=%async_computation | async-start | bytes 524288 | tf_op jit(solution)/shard_map/all_to_all | solution.py:44
  161.4 201.9 %all-gather.15.cloned.1.call-start = ((), (), s32[]{:S(2)}) async-start(), calls=%async_computation.4 | async-start | bytes 2621440 | tf_op jit(solution)/shard_map/all_gather | solution.py:31
  372.1 71.9 %all-to-all-start.1 = ((f32[4,32,512]{2,1,0:T(8,128)}), f32[4,32,512]{2,1,0:T(8,128)S(1)}, u32[]{:S(2)}, u32[]{:S(2)}) async-start(f32[4,32,512]{2,1,0:T(8,128)} %broadcast_in_dim.12), calls=%async_computation.1 | async-start | bytes 524288 | tf_op jit(solution)/shard_map/all_to_all | solution.py:44
  376.3 236.4 %all-gather.17.cloned.1.call-start = ((), (), s32[]{:S(2)}) async-start(), calls=%async_computation.5 | async-start | bytes 2621440 | tf_op jit(solution)/shard_map/all_gather | solution.py:31
  621.4 8.8 %all-to-all-start.2 = ((f32[4,32,512]{2,1,0:T(8,128)}), f32[4,32,512]{2,1,0:T(8,128)S(1)}, u32[]{:S(2)}, u32[]{:S(2)}) async-start(f32[4,32,512]{2,1,0:T(8,128)} %broadcast_in_dim.13), calls=%async_computation.2 | async-start | bytes 524288 | tf_op jit(solution)/shard_map/all_to_all | solution.py:44
Sparse Core Ops, SparseCore 0:
  115.3 34.5 all-gather.12
  326.6 36.7 all-gather.14
  541.4 36.7 all-gather.16
where the time goes:
time: 712 us; the launch traced here: 711 us
  blocking collectives  548 us (77%)
  waiting for transfers between devices  75.4 us (11%)
  other arithmetic  29.6 us (4%)
  matrix products  19.3 us (3%)
  between operations  14.2 us (2%)
  local copies, waits for them, and re-layouts  12 us (2%)
  starting transfers between devices  12 us (2%)
    psum x35, blocking collectives, one_axis_at_a_time(): shard = lax.psum(shard, axis)  468 us
    all_gather x6, blocking collectives, all_blocks(): parts = lax.all_gather(parts, axes[k])  79.7 us
    all_gather x3, waiting for transfers between devices, all_blocks(): parts = lax.all_gather(parts, axes[k])  70.1 us
    dot_general x3, matrix products, local(): lax.dot_general(col_block, operator, (((1,), (1,)), ((), ())), preferred_...  14.6 us
  transfers between devices with their start and end apart: 6, of which 3 were waited for; matrix products, arithmetic and copies ran while one was open for 0% of the time, Pallas kernels for 0%

commit v1 on v0

--- a/solution.py
+++ b/solution.py
@@ -15,7 +15,7 @@
 
 def one_axis_at_a_time(shard, axes):
     for axis in axes:
-        shard = lax.psum(shard, axis)
+        shard = jnp.sum(lax.all_gather(shard, axis), axis=0)
     return shard
 
 

time: 712 us -> 752 us (1.056)
  blocking collectives: 548 us -> 581 us
    all_gather x0 -> x50, blocking collectives: none -> 502 us  [one_axis_at_a_time(): shard = jnp.sum(lax.all_gather(shard, axis), axis=0)]
    psum x35 -> x0, blocking collectives: 468 us -> none  [one_axis_at_a_time(): shard = lax.psum(shard, axis)]
where the time goes in v1:
time: 752 us; the launch traced here: 751 us
  blocking collectives  581 us (77%)
  waiting for transfers between devices  82.3 us (11%)
  other arithmetic  29.5 us (4%)
  matrix products  19.3 us (3%)
  between operations  14.3 us (2%)
  starting transfers between devices  12.2 us (2%)
  local copies, waits for them, and re-layouts  11.7 us (2%)
    all_gather x50, blocking collectives, one_axis_at_a_time(): shard = jnp.sum(lax.all_gather(shard, axis), axis=0)  502 us
    all_gather x6, blocking collectives, all_blocks(): parts = lax.all_gather(parts, axes[k])  79.5 us
    all_gather x3, waiting for transfers between devices, all_blocks(): parts = lax.all_gather(parts, axes[k])  77.2 us
  transfers between devices with their start and end apart: 6, of which 3 were waited for; matrix products, arithmetic and copies ran while one was open for 0% of the time, Pallas kernels for 0%

profile of v1, /device:TPU:1, one launch (start us, length us, event | category | flops | bytes accessed | tf_op | source)
XLA Modules:
  0.0 750.6 jit_solution(16564965115281183012)
XLA Ops:
  8.2 10.4 %all-gather = f32[128,32]{1,0:T(8,128)S(1)} all-gather(f32[32,32]{1,0:T(8,128)S(1)} %fusion.48), channel_id=2, replica_groups=mesh['row_0'=4,'row_1'=2,'row_2'=8,'col_0'=2,'col_1'=2] {'row_0'}, dimensions={0}, use_global_device_ids=true | all-gather | bytes 20480 | tf_op jit(solution)/shard_map/all_gather | solution.py:18
  23.3 21.9 %all-gather.2 = f32[256,32]{1,0:T(8,128)S(1)} all-gather(f32[32,32]{1,0:T(8,128)S(1)} %reduce_sum.478), channel_id=4, replica_groups=mesh['row_0'=4,'row_1'=2,'row_2'=8,'col_0'=2,'col_1'=2] {'row_2'}, dimensions={0}, use_global_device_ids=true | all-gather | bytes 36864 | tf_op jit(solution)/shard_map/all_gather | solution.py:18
  48.8 13.3 %all-gather.4 = f32[64,32]{1,0:T(8,128)S(1)} all-gather(f32[32,32]{1,0:T(8,128)S(1)} %reduce_sum.480), channel_id=6, replica_groups=mesh['row_0'=4,'row_1'=2,'row_2'=8,'col_0'=2,'col_1'=2] {'col_1'}, dimensions={0}, use_global_device_ids=true | all-gather | bytes 12288 | tf_op jit(solution)/shard_map/all_gather | solution.py:18
  74.8 21.7 %all-gather.6 = bf16[16,32,512]{2,1,0:T(8,128)(2,1)} all-gather(bf16[2,32,512]{2,1,0:T(8,128)(2,1)S(1)} %bitcast.166), channel_id=8, replica_groups=mesh['row_0'=4,'row_1'=2,'row_2'=8,'col_0'=2,'col_1'=2] {'row_2'}, dimensions={0}, use_global_device_ids=true | all-gather | bytes 589824 | tf_op jit(solution)/shard_map/all_gather | solution.py:31
  96.8 38.4 %all-gather.73.cloned.1.call-done = bf16[32,2,32,512]{3,2,1,0:T(8,128)(2,1)} async-done(((bf16[8,2,32,512]{3,2,1,0:T(8,128)(2,1)}), bf16[32,2,32,512]{3,2,1,0:T(8,128)(2,1)}) %all-gather.73.cloned.1.call-update) | async-done | bytes 2097168 | tf_op jit(solution)/shard_map/all_gather | solution.py:31
  146.8 9.0 %all-gather.8 = f32[128,64]{1,0:T(8,128)S(1)} all-gather(f32[32,64]{1,0:T(8,128)S(1)} %fusion.22), channel_id=10, replica_groups=mesh['row_0'=4,'row_1'=2,'row_2'=8,'col_0'=2,'col_1'=2] {'row_0'}, dimensions={0}, use_global_device_ids=true | all-gather | bytes 40960 | tf_op jit(solution)/shard_map/all_gather | solution.py:18
  160.6 20.0 %all-gather.10 = f32[256,64]{1,0:T(8,128)S(1)} all-gather(f32[32,64]{1,0:T(8,128)S(1)} %reduce_sum.484), channel_id=12, replica_groups=mesh['row_0'=4,'row_1'=2,'row_2'=8,'col_0'=2,'col_1'=2] {'row_2'}, dimensions={0}, use_global_device_ids=true | all-gather | bytes 73728 | tf_op jit(solution)/shard_map/all_gather | solution.py:18
  184.1 12.7 %all-gather.12 = f32[64,64]{1,0:T(8,128)S(1)} all-gather(f32[32,64]{1,0:T(8,128)S(1)} %reduce_sum.486), channel_id=14, replica_groups=mesh['row_0'=4,'row_1'=2,'row_2'=8,'col_0'=2,'col_1'=2] {'col_1'}, dimensions={0}, use_global_device_ids=true | all-gather | bytes 24576 | tf_op jit(solution)/shard_map/all_gather | solution.py:18
  211.2 18.5 %all-gather.20 = f32[256,32]{1,0:T(8,128)S(1)} all-gather(f32[32,32]{1,0:T(8,128)S(1)} %reduce_sum.494), channel_id=22, replica_groups=mesh['row_0'=4,'row_1'=2,'row_2'=8,'col_0'=2,'col_1'=2] {'row_2'}, dimensions={0}, use_global_device_ids=true | all-gather | bytes 36864 | tf_op jit(solution)/shard_map/all_gather | solution.py:18
  233.5 12.7 %all-gather.22 = f32[64,32]{1,0:T(8,128)S(1)} all-gather(f32[32,32]{1,0:T(8,128)S(1)} %reduce_sum.496), channel_id=24, replica_groups=mesh['row_0'=4,'row_1'=2,'row_2'=8,'col_0'=2,'col_1'=2] {'col_1'}, dimensions={0}, use_global_device_ids=true | all-gather | bytes 12288 | tf_op jit(solution)/shard_map/all_gather | solution.py:18
  246.4 9.0 %all-gather.13 = f32[128,32]{1,0:T(8,128)S(1)} all-gather(f32[32,32]{1,0:T(8,128)S(1)} %fusion.57), channel_id=15, replica_groups=mesh['row_0'=4,'row_1'=2,'row_2'=8,'col_0'=2,'col_1'=2] {'row_0'}, dimensions={0}, use_global_device_ids=true | all-gather | bytes 20480 | tf_op jit(solution)/shard_map/all_gather | solution.py:18
  260.2 18.5 %all-gather.15 = f32[256,32]{1,0:T(8,128)S(1)} all-gather(f32[32,32]{1,0:T(8,128)S(1)} %reduce_sum.489), channel_id=17, replica_groups=mesh['row_0'=4,'row_1'=2,'row_2'=8,'col_0'=2,'col_1'=2] {'row_2'}, dimensions={0}, use_global_device_ids=true | all-gather | bytes 36864 | tf_op jit(solution)/shard_map/all_gather | solution.py:18
  282.4 12.7 %all-gather.17 = f32[64,32]{1,0:T(8,128)S(1)} all-gather(f32[32,32]{1,0:T(8,128)S(1)} %reduce_sum.491), channel_id=19, replica_groups=mesh['row_0'=4,'row_1'=2,'row_2'=8,'col_0'=2,'col_1'=2] {'col_1'}, dimensions={0}, use_global_device_ids=true | all-gather | bytes 12288 | tf_op jit(solution)/shard_map/all_gather | solution.py:18
  307.3 21.5 %all-gather.24 = bf16[16,32,512]{2,1,0:T(8,128)(2,1)} all-gather(bf16[2,32,512]{2,1,0:T(8,128)(2,1)S(1)} %bitcast.167), channel_id=26, replica_groups=mesh['row_0'=4,'row_1'=2,'row_2'=8,'col_0'=2,'col_1'=2] {'row_2'}, dimensions={0}, use_global_device_ids=true | all-gather | bytes 589824 | tf_op jit(solution)/shard_map/all_gather | solution.py:31
  328.8 38.9 %all-gather.75.cloned.1.call-done = bf16[32,2,32,512]{3,2,1,0:T(8,128)(2,1)} async-done(((bf16[8,2,32,512]{3,2,1,0:T(8,128)(2,1)}), bf16[32,2,32,512]{3,2,1,0:T(8,128)(2,1)}) %all-gather.75.cloned.1.call-update) | async-done | bytes 2097168 | tf_op jit(solution)/shard_map/all_gather | solution.py:31
  380.8 9.0 %all-gather.26 = f32[128,64]{1,0:T(8,128)S(1)} all-gather(f32[32,64]{1,0:T(8,128)S(1)} %fusion.20), channel_id=28, replica_groups=mesh['row_0'=4,'row_1'=2,'row_2'=8,'col_0'=2,'col_1'=2] {'row_0'}, dimensions={0}, use_global_device_ids=true | all-gather | bytes 40960 | tf_op jit(solution)/shard_map/all_gather | solution.py:18
  394.6 20.0 %all-gather.28 = f32[256,64]{1,0:T(8,128)S(1)} all-gather(f32[32,64]{1,0:T(8,128)S(1)} %reduce_sum.500), channel_id=30, replica_groups=mesh['row_0'=4,'row_1'=2,'row_2'=8,'col_0'=2,'col_1'=2] {'row_2'}, dimensions={0}, use_global_device_ids=true | all-gather | bytes 73728 | tf_op jit(solution)/shard_map/all_gather | solution.py:18
  418.1 12.7 %all-gather.30 = f32[64,64]{1,0:T(8,128)S(1)} all-gather(f32[32,64]{1,0:T(8,128)S(1)} %reduce_sum.502), channel_id=32, replica_groups=mesh['row_0'=4,'row_1'=2,'row_2'=8,'col_0'=2,'col_1'=2] {'col_1'}, dimensions={0}, use_global_device_ids=true | all-gather | bytes 24576 | tf_op jit(solution)/shard_map/all_gather | solution.py:18
  445.2 18.5 %all-gather.61 = f32[8,64,32]{1,2,0:T(8,128)S(1)} all-gather(f32[1,64,32]{1,2,0:T(8,128)S(1)} %bitcast.194), channel_id=40, replica_groups=mesh['row_0'=4,'row_1'=2,'row_2'=8,'col_0'=2,'col_1'=2] {'row_2'}, dimensions={0}, use_global_device_ids=true | all-gather | bytes 73728 | tf_op jit(solution)/shard_map/all_gather | solution.py:18
  467.4 12.7 %all-gather.63 = f32[2,64,32]{1,2,0:T(8,128)S(1)} all-gather(f32[1,64,32]{1,2,0:T(8,128)S(1)} %bitcast.196), channel_id=42, replica_groups=mesh['row_0'=4,'row_1'=2,'row_2'=8,'col_0'=2,'col_1'=2] {'col_1'}, dimensions={0}, use_global_device_ids=true | all-gather | bytes 24576 | tf_op jit(solution)/shard_map/all_gather | solution.py:18
  480.3 9.0 %all-gather.31 = f32[128,32]{1,0:T(8,128)S(1)} all-gather(f32[32,32]{1,0:T(8,128)S(1)} %fusion.54), channel_id=33, replica_groups=mesh['row_0'=4,'row_1'=2,'row_2'=8,'col_0'=2,'col_1'=2] {'row_0'}, dimensions={0}, use_global_device_ids=true | all-gather | bytes 20480 | tf_op jit(solution)/shard_map/all_gather | solution.py:18
  494.1 18.7 %all-gather.33 = f32[256,32]{1,0:T(8,128)S(1)} all-gather(f32[32,32]{1,0:T(8,128)S(1)} %reduce_sum.505), channel_id=35, replica_groups=mesh['row_0'=4,'row_1'=2,'row_2'=8,'col_0'=2,'col_1'=2] {'row_2'}, dimensions={0}, use_global_device_ids=true | all-gather | bytes 36864 | tf_op jit(solution)/shard_map/all_gather | solution.py:18
  516.5 12.7 %all-gather.35 = f32[64,32]{1,0:T(8,128)S(1)} all-gather(f32[32,32]{1,0:T(8,128)S(1)} %reduce_sum.507), channel_id=37, replica_groups=mesh['row_0'=4,'row_1'=2,'row_2'=8,'col_0'=2,'col_1'=2] {'col_1'}, dimensions={0}, use_global_device_ids=true | all-gather | bytes 12288 | tf_op jit(solution)/shard_map/all_gather | solution.py:18
  541.4 21.5 %all-gather.42 = bf16[16,32,512]{2,1,0:T(8,128)(2,1)} all-gather(bf16[2,32,512]{2,1,0:T(8,128)(2,1)S(1)} %bitcast.168), channel_id=44, replica_groups=mesh['row_0'=4,'row_1'=2,'row_2'=8,'col_0'=2,'col_1'=2] {'row_2'}, dimensions={0}, use_global_device_ids=true | all-gather | bytes 589824 | tf_op jit(solution)/shard_map/all_gather | solution.py:31
  563.0 9.0 %all-gather.44 = f32[128,64]{1,0:T(8,128)S(1)} all-gather(f32[32,64]{1,0:T(8,128)S(1)} %fusion.18), channel_id=46, replica_groups=mesh['row_0'=4,'row_1'=2,'row_2'=8,'col_0'=2,'col_1'=2] {'row_0'}, dimensions={0}, use_global_device_ids=true | all-gather | bytes 40960 | tf_op jit(solution)/shard_map/all_gather | solution.py:18
  576.8 20.2 %all-gather.46 = f32[256,64]{1,0:T(8,128)S(1)} all-gather(f32[32,64]{1,0:T(8,128)S(1)} %reduce_sum.516), channel_id=48, replica_groups=mesh['row_0'=4,'row_1'=2,'row_2'=8,'col_0'=2,'col_1'=2] {'row_2'}, dimensions={0}, use_global_device_ids=true | all-gather | bytes 73728 | tf_op jit(solution)/shard_map/all_gather | solution.py:18
  600.9 18.0 %all-gather.48 = f32[64,64]{1,0:T(8,128)S(1)} all-gather(f32[32,64]{1,0:T(8,128)S(1)} %reduce_sum.518), channel_id=50, replica_groups=mesh['row_0'=4,'row_1'=2,'row_2'=8,'col_0'=2,'col_1'=2] {'col_1'}, dimensions={0}, use_global_device_ids=true | all-gather | bytes 24576 | tf_op jit(solution)/shard_map/all_gather | solution.py:18
  637.2 9.0 %all-gather.64 = f32[4,96,32]{1,2,0:T(8,128)S(1)} all-gather(f32[1,96,32]{1,2,0:T(8,128)S(1)} %convolution_bitcast_fusion), channel_id=56, replica_groups=mesh['row_0'=4,'row_1'=2,'row_2'=8,'col_0'=2,'col_1'=2] {'row_0'}, dimensions={0}, use_global_device_ids=true | all-gather | bytes 61440 | tf_op jit(solution)/shard_map/all_gather | solution.py:18
  650.9 18.8 %all-gather.66 = f32[8,96,32]{1,2,0:T(8,128)S(1)} all-gather(f32[1,96,32]{1,2,0:T(8,128)S(1)} %bitcast.198), channel_id=58, replica_groups=mesh['row_0'=4,'row_1'=2,'row_2'=8,'col_0'=2,'col_1'=2] {'row_2'}, dimensions={0}, use_global_device_ids=true | all-gather | bytes 110592 | tf_op jit(solution)/shard_map/all_gather | solution.py:18
  673.3 13.2 %all-gather.68 = f32[2,96,32]{1,2,0:T(8,128)S(1)} all-gather(f32[1,96,32]{1,2,0:T(8,128)S(1)} %bitcast.200), channel_id=60, replica_groups=mesh['row_0'=4,'row_1'=2,'row_2'=8,'col_0'=2,'col_1'=2] {'col_1'}, dimensions={0}, use_global_device_ids=true | all-gather | bytes 36864 | tf_op jit(solution)/shard_map/all_gather | solution.py:18
  700.5 18.3 %all-gather.51 = f32[256,32]{1,0:T(8,128)S(1)} all-gather(f32[32,32]{1,0:T(8,128)S(1)} %reduce_sum.521), channel_id=53, replica_groups=mesh['row_0'=4,'row_1'=2,'row_2'=8,'col_0'=2,'col_1'=2] {'row_2'}, dimensions={0}, use_global_device_ids=true | all-gather | bytes 36864 | tf_op jit(solution)/shard_map/all_gather | solution.py:18
  722.4 13.1 %all-gather.53 = f32[64,32]{1,0:T(8,128)S(1)} all-gather(f32[32,32]{1,0:T(8,128)S(1)} %reduce_sum.523), channel_id=55, replica_groups=mesh['row_0'=4,'row_1'=2,'row_2'=8,'col_0'=2,'col_1'=2] {'col_1'}, dimensions={0}, use_global_device_ids=true | all-gather | bytes 12288 | tf_op jit(solution)/shard_map/all_gather | solution.py:18
  (179 shorter events, 203.3 us)
Async XLA Ops:
  7.2 0.8 copy-start
  7.2 89.4 %copy-start.3 = (f32[512]{0:T(512)S(1)}, f32[512]{0:T(512)}, u32[]{:S(2)}) copy-start(f32[512]{0:T(512)} %param.10) | copy-start | bytes 6148
  7.2 89.5 %copy-start.2 = (s32[512]{0:T(512)S(1)}, s32[512]{0:T(512)}, u32[]{:S(2)}) copy-start(s32[512]{0:T(512)} %param.9) | copy-start | bytes 6148
  7.2 128.0 %all-gather.73.cloned.1.call-start = ((), (), s32[]{:S(2)}) async-start(), calls=%async_computation.3 | async-start | bytes 2621440 | tf_op jit(solution)/shard_map/all_gather | solution.py:31
  135.2 4.0 copy-start.1
  142.5 54.3 %all-to-all-start = ((f32[4,32,512]{2,1,0:T(8,128)}), f32[4,32,512]{2,1,0:T(8,128)S(1)}, u32[]{:S(2)}, u32[]{:S(2)}) async-start(f32[4,32,512]{2,1,0:T(8,128)} %broadcast_in_dim.11), calls=%async_computation | async-start | bytes 524288 | tf_op jit(solution)/shard_map/all_to_all | solution.py:44
  146.7 221.0 %all-gather.75.cloned.1.call-start = ((), (), s32[]{:S(2)}) async-start(), calls=%async_computation.4 | async-start | bytes 2621440 | tf_op jit(solution)/shard_map/all_gather | solution.py:31
  376.4 54.3 %all-to-all-start.1 = ((f32[4,32,512]{2,1,0:T(8,128)}), f32[4,32,512]{2,1,0:T(8,128)S(1)}, u32[]{:S(2)}, u32[]{:S(2)}) async-start(f32[4,32,512]{2,1,0:T(8,128)} %broadcast_in_dim.12), calls=%async_computation.1 | async-start | bytes 524288 | tf_op jit(solution)/shard_map/all_to_all | solution.py:44
  380.6 238.3 %all-gather.77.cloned.1.call-start = ((), (), s32[]{:S(2)}) async-start(), calls=%async_computation.5 | async-start | bytes 2621440 | tf_op jit(solution)/shard_map/all_gather | solution.py:31
  627.7 8.8 %all-to-all-start.2 = ((f32[4,32,512]{2,1,0:T(8,128)}), f32[4,32,512]{2,1,0:T(8,128)S(1)}, u32[]{:S(2)}, u32[]{:S(2)}) async-start(f32[4,32,512]{2,1,0:T(8,128)} %broadcast_in_dim.13), calls=%async_computation.2 | async-start | bytes 524288 | tf_op jit(solution)/shard_map/all_to_all | solution.py:44
Sparse Core Ops, SparseCore 0:
  96.7 38.4 all-gather.72
  329.0 38.6 all-gather.74
  563.0 38.6 all-gather.76
